TPU v7x, 128 devices: a whole 4x4x4 slice. The times are simulated.
128 devices in a mesh: smp: 8 (over x_lo, z), bld: 16 (over y, x_hi, core).
Axes of the slice: x: 4 (x_hi: 2, x_lo: 2; x = x_hi * 2 + x_lo), y: 4, z: 4, core: 2. Of those that a mesh axis runs over, the one named last changes fastest.
Arguments:
- tensor: bfloat16 [4, 8192, 16384], P(None, 'smp', 'bld'), may hold values from -576 to 576
- building_factor: float32 [64, 16384], P(None, 'bld'), may hold values from -144 to 144
- hour_weights: float32 [4, 64], replicated, may hold values from -5 to 5
Outputs:
- sample_factor: float32 [64, 8192], P(None, ('smp', 'bld'))
- building_out: float32 [64, 16384], P(None, ('bld', 'smp'))
- hour_out: float32 [4, 64], replicated
All inputs are finite; a program needn't handle non-finite values.
Results may differ from a plain program's by a relative error of at most 0.008.
Values may be sent and summed in bfloat16 or wider, within the bound.
A program may use at most 64 MiB of HBM per device.

v0:
```python
import math
import jax
import jax.numpy as jnp
from jax import lax
from jax.sharding import PartitionSpec as P

SWEEPS = 5
EPSILON = 1e-06
RIDGE_SHARE = 0.05


def regularized(gram):
    order_size = gram.shape[0]
    return gram + RIDGE_SHARE * jnp.mean(jnp.diagonal(gram)) * jnp.eye(order_size, dtype=gram.dtype)


def solve_rows(gram, right_side):
    lower_factor = jnp.linalg.cholesky(regularized(gram))
    middle = lax.linalg.triangular_solve(lower_factor, right_side, left_side=True, lower=True)
    return lax.linalg.triangular_solve(
        lower_factor, middle, left_side=True, lower=True, transpose_a=True
    )


def finish(unscaled, gram_raw, row_count):
    column_norm = jnp.sqrt(jnp.diagonal(gram_raw) / row_count + EPSILON)
    return (
        unscaled / column_norm[:, None],
        gram_raw / (column_norm[:, None] * column_norm[None, :]),
    )


def hour_gram(hourly):
    return jnp.dot(hourly.T, hourly, precision=lax.Precision.HIGHEST)


def self_gram(unscaled):
    return jnp.dot(unscaled, unscaled.T, precision=lax.Precision.HIGHEST)


def local(tensor, building_factor, hour_weights):
    samples_total = tensor.shape[1] * lax.axis_size("smp")
    buildings_total = tensor.shape[2] * lax.axis_size("bld")
    scale_up = math.sqrt(samples_total * buildings_total)
    hourly = hour_weights / scale_up
    gram_build = lax.psum(self_gram(building_factor), "bld")
    build_low = building_factor.astype(jnp.bfloat16)
    partial_value = jnp.einsum("rj,kij->kri", build_low, tensor, preferred_element_type=jnp.float32)
    sample_out = None
    building_out = None
    for sweep_index in range(SWEEPS):
        sample_terms = jnp.sum(hourly[:, :, None] * partial_value, axis=0)
        sample_rhs = lax.psum(sample_terms, "bld")
        unscaled = solve_rows(gram_build * hour_gram(hourly), sample_rhs)
        gram_raw = lax.psum(self_gram(unscaled), "smp")
        samples_now, gram_sample = finish(unscaled, gram_raw, samples_total)
        sample_low = samples_now.astype(jnp.bfloat16)
        share_width = samples_now.shape[1] // lax.axis_size("bld")
        sample_out = lax.dynamic_slice_in_dim(
            samples_now, lax.axis_index("bld") * share_width, share_width, 1
        )
        mixed = jnp.einsum("ri,kij->krj", sample_low, tensor, preferred_element_type=jnp.float32)
        build_terms = jnp.sum(hourly[:, :, None] * mixed, axis=0)
        build_rhs = lax.psum(build_terms, "smp")
        unscaled = solve_rows(gram_sample * hour_gram(hourly), build_rhs)
        gram_raw = lax.psum(self_gram(unscaled), "bld")
        building_now, gram_build = finish(unscaled, gram_raw, buildings_total)
        build_low = building_now.astype(jnp.bfloat16)
        share_width = building_now.shape[1] // lax.axis_size("smp")
        building_out = lax.dynamic_slice_in_dim(
            building_now, lax.axis_index("smp") * share_width, share_width, 1
        )
        partial_value = jnp.einsum(
            "rj,kij->kri", build_low, tensor, preferred_element_type=jnp.float32
        )
        hour_terms = jnp.sum(sample_low.astype(jnp.float32)[None, :, :] * partial_value, axis=2)
        hour_rhs = lax.psum(hour_terms, ("smp", "bld"))
        hourly = solve_rows(gram_sample * gram_build, hour_rhs.T).T
    return (sample_out, building_out, hourly * scale_up)


def solution(mesh):
    in_specs = (P(None, "smp", "bld"), P(None, "bld"), P())
    out_specs = (P(None, ("smp", "bld")), P(None, ("bld", "smp")), P())
    return jax.shard_map(local, mesh=mesh, in_specs=in_specs, out_specs=out_specs, check_vma=False)
```

profile of v0, /device:TPU:1, one launch (start us, length us, event | category | flops | bytes accessed | tf_op | source)
XLA Modules:
  0.0 2094.5 jit_solution(17855161390660669668)
XLA Ops:
  8.0 6.7 fusion.10
  15.2 65.3 %psum.182 = f32[64,64]{0,1:T(8,128)S(1)} all-reduce(f32[64,64]{0,1:T(8,128)S(1)} %fusion.159), channel_id=1, replica_groups=mesh['smp'=8,'bld'=16] {'bld'}, use_global_device_ids=true, to_apply=%region_0.0 | all-reduce | flops 4096 | bytes 32768 | tf_op jit(solution)/shard_map/psum | solution.py:46
  95.0 60.6 %all-reduce.11.cloned.1.call-done = f32[64,1024]{1,0:T(8,128)} async-done(((f32[64,1024]{1,0:T(8,128)}), f32[64,1024]{1,0:T(8,128)}) %all-reduce.11.cloned.1.call-update) | async-done | bytes 262160 | tf_op jit(solution)/shard_map/psum | solution.py:53
  157.7 26.2 %psum.184 = f32[64,64]{0,1:T(8,128)S(1)} all-reduce(f32[64,64]{0,1:T(8,128)S(1)} %fusion.160), channel_id=1, replica_groups=mesh['smp'=8,'bld'=16] {'smp'}, use_global_device_ids=true, to_apply=%region_6.10 | all-reduce | flops 4096 | bytes 32768 | tf_op jit(solution)/shard_map/psum | solution.py:55
  205.1 65.8 %all-reduce.13.cloned.1.call-done = f32[64,1024]{1,0:T(8,128)} async-done(((f32[64,1024]{1,0:T(8,128)}), f32[64,1024]{1,0:T(8,128)}) %all-reduce.13.cloned.1.call-update) | async-done | bytes 262160 | tf_op jit(solution)/shard_map/psum | solution.py:64
  273.0 65.3 %psum.186 = f32[64,64]{0,1:T(8,128)S(1)} all-reduce(f32[64,64]{0,1:T(8,128)S(1)} %fusion.161), channel_id=1, replica_groups=mesh['smp'=8,'bld'=16] {'bld'}, use_global_device_ids=true, to_apply=%region_10.14 | all-reduce | flops 4096 | bytes 32768 | tf_op jit(solution)/shard_map/psum | solution.py:66
  353.5 6.2 multiply_reduce_fusion.7
  359.6 67.3 %psum.187 = f32[64,4]{0,1:T(4,128)S(1)} all-reduce(f32[64,4]{0,1:T(4,128)S(1)} %bitcast.367), channel_id=1, replica_groups=mesh['smp'=8,'bld'=16] {'smp','bld'}, use_global_device_ids=true, to_apply=%region_13.17 | all-reduce | flops 256 | bytes 2048 | tf_op jit(solution)/shard_map/psum | solution.py:77
  442.7 127.8 %all-reduce.15.cloned.1.call-done = f32[64,1024]{1,0:T(8,128)} async-done(((f32[64,1024]{1,0:T(8,128)}), f32[64,1024]{1,0:T(8,128)}) %all-reduce.15.cloned.1.call-update) | async-done | bytes 262160 | tf_op jit(solution)/shard_map/psum | solution.py:53
  572.6 26.5 %psum.189 = f32[64,64]{0,1:T(8,128)S(1)} all-reduce(f32[64,64]{0,1:T(8,128)S(1)} %fusion.162), channel_id=1, replica_groups=mesh['smp'=8,'bld'=16] {'smp'}, use_global_device_ids=true, to_apply=%region_17.23 | all-reduce | flops 4096 | bytes 32768 | tf_op jit(solution)/shard_map/psum | solution.py:55
  620.2 65.8 %all-reduce.17.cloned.1.call-done = f32[64,1024]{1,0:T(8,128)} async-done(((f32[64,1024]{1,0:T(8,128)}), f32[64,1024]{1,0:T(8,128)}) %all-reduce.17.cloned.1.call-update) | async-done | bytes 262160 | tf_op jit(solution)/shard_map/psum | solution.py:64
  688.1 64.7 %psum.191 = f32[64,64]{0,1:T(8,128)S(1)} all-reduce(f32[64,64]{0,1:T(8,128)S(1)} %fusion.163), channel_id=1, replica_groups=mesh['smp'=8,'bld'=16] {'bld'}, use_global_device_ids=true, to_apply=%region_21.27 | all-reduce | flops 4096 | bytes 32768 | tf_op jit(solution)/shard_map/psum | solution.py:66
  768.0 6.2 multiply_reduce_fusion.5
  774.2 67.5 %psum.192 = f32[64,4]{0,1:T(4,128)S(1)} all-reduce(f32[64,4]{0,1:T(4,128)S(1)} %bitcast.368), channel_id=1, replica_groups=mesh['smp'=8,'bld'=16] {'smp','bld'}, use_global_device_ids=true, to_apply=%region_24.30 | all-reduce | flops 256 | bytes 2048 | tf_op jit(solution)/shard_map/psum | solution.py:77
  857.5 127.8 %all-reduce.19.cloned.1.call-done = f32[64,1024]{1,0:T(8,128)} async-done(((f32[64,1024]{1,0:T(8,128)}), f32[64,1024]{1,0:T(8,128)}) %all-reduce.19.cloned.1.call-update) | async-done | bytes 262160 | tf_op jit(solution)/shard_map/psum | solution.py:53
  987.4 26.2 %psum.194 = f32[64,64]{0,1:T(8,128)S(1)} all-reduce(f32[64,64]{0,1:T(8,128)S(1)} %fusion.164), channel_id=1, replica_groups=mesh['smp'=8,'bld'=16] {'smp'}, use_global_device_ids=true, to_apply=%region_28.34 | all-reduce | flops 4096 | bytes 32768 | tf_op jit(solution)/shard_map/psum | solution.py:55
  1034.7 65.8 %all-reduce.21.cloned.1.call-done = f32[64,1024]{1,0:T(8,128)} async-done(((f32[64,1024]{1,0:T(8,128)}), f32[64,1024]{1,0:T(8,128)}) %all-reduce.21.cloned.1.call-update) | async-done | bytes 262160 | tf_op jit(solution)/shard_map/psum | solution.py:64
  1102.6 65.2 %psum.196 = f32[64,64]{0,1:T(8,128)S(1)} all-reduce(f32[64,64]{0,1:T(8,128)S(1)} %fusion.165), channel_id=1, replica_groups=mesh['smp'=8,'bld'=16] {'bld'}, use_global_device_ids=true, to_apply=%region_32.38 | all-reduce | flops 4096 | bytes 32768 | tf_op jit(solution)/shard_map/psum | solution.py:66
  1182.9 6.2 multiply_reduce_fusion.3
  1189.1 67.3 %psum.197 = f32[64,4]{0,1:T(4,128)S(1)} all-reduce(f32[64,4]{0,1:T(4,128)S(1)} %bitcast.369), channel_id=1, replica_groups=mesh['smp'=8,'bld'=16] {'smp','bld'}, use_global_device_ids=true, to_apply=%region_35.41 | all-reduce | flops 256 | bytes 2048 | tf_op jit(solution)/shard_map/psum | solution.py:77
  1272.2 127.8 %all-reduce.23.cloned.1.call-done = f32[64,1024]{1,0:T(8,128)} async-done(((f32[64,1024]{1,0:T(8,128)}), f32[64,1024]{1,0:T(8,128)}) %all-reduce.23.cloned.1.call-update) | async-done | bytes 262160 | tf_op jit(solution)/shard_map/psum | solution.py:53
  1402.0 26.5 %psum.199 = f32[64,64]{0,1:T(8,128)S(1)} all-reduce(f32[64,64]{0,1:T(8,128)S(1)} %fusion.166), channel_id=1, replica_groups=mesh['smp'=8,'bld'=16] {'smp'}, use_global_device_ids=true, to_apply=%region_39.45 | all-reduce | flops 4096 | bytes 32768 | tf_op jit(solution)/shard_map/psum | solution.py:55
  1449.7 65.8 %all-reduce.25.cloned.1.call-done = f32[64,1024]{1,0:T(8,128)} async-done(((f32[64,1024]{1,0:T(8,128)}), f32[64,1024]{1,0:T(8,128)}) %all-reduce.25.cloned.1.call-update) | async-done | bytes 262160 | tf_op jit(solution)/shard_map/psum | solution.py:64
  1517.6 64.7 %psum.201 = f32[64,64]{0,1:T(8,128)S(1)} all-reduce(f32[64,64]{0,1:T(8,128)S(1)} %fusion.167), channel_id=1, replica_groups=mesh['smp'=8,'bld'=16] {'bld'}, use_global_device_ids=true, to_apply=%region_43.49 | all-reduce | flops 4096 | bytes 32768 | tf_op jit(solution)/shard_map/psum | solution.py:66
  1597.5 6.2 multiply_reduce_fusion.1
  1603.6 67.5 %psum.202 = f32[64,4]{0,1:T(4,128)S(1)} all-reduce(f32[64,4]{0,1:T(4,128)S(1)} %bitcast.370), channel_id=1, replica_groups=mesh['smp'=8,'bld'=16] {'smp','bld'}, use_global_device_ids=true, to_apply=%region_46.52 | all-reduce | flops 256 | bytes 2048 | tf_op jit(solution)/shard_map/psum | solution.py:77
  1686.9 127.8 %all-reduce.27.cloned.1.call-done = f32[64,1024]{1,0:T(8,128)} async-done(((f32[64,1024]{1,0:T(8,128)}), f32[64,1024]{1,0:T(8,128)}) %all-reduce.27.cloned.1.call-update) | async-done | bytes 262160 | tf_op jit(solution)/shard_map/psum | solution.py:53
  1816.8 26.2 %psum.204 = f32[64,64]{0,1:T(8,128)S(1)} all-reduce(f32[64,64]{0,1:T(8,128)S(1)} %fusion.168), channel_id=1, replica_groups=mesh['smp'=8,'bld'=16] {'smp'}, use_global_device_ids=true, to_apply=%region_50.56 | all-reduce | flops 4096 | bytes 32768 | tf_op jit(solution)/shard_map/psum | solution.py:55
  1864.7 65.3 %all-reduce.29.cloned.1.call-done = f32[64,1024]{1,0:T(8,128)} async-done(((f32[64,1024]{1,0:T(8,128)}), f32[64,1024]{1,0:T(8,128)}) %all-reduce.29.cloned.1.call-update) | async-done | bytes 262160 | tf_op jit(solution)/shard_map/psum | solution.py:64
  1932.1 65.0 %psum.206 = f32[64,64]{0,1:T(8,128)S(1)} all-reduce(f32[64,64]{0,1:T(8,128)S(1)} %fusion.169), channel_id=1, replica_groups=mesh['smp'=8,'bld'=16] {'bld'}, use_global_device_ids=true, to_apply=%region_54.60 | all-reduce | flops 4096 | bytes 32768 | tf_op jit(solution)/shard_map/psum | solution.py:66
  2012.4 6.2 fusion.11
  2018.5 67.3 %psum.207 = f32[64,4]{0,1:T(4,128)S(1)} all-reduce(f32[64,4]{0,1:T(4,128)S(1)} %fusion.11), channel_id=1, replica_groups=mesh['smp'=8,'bld'=16] {'smp','bld'}, use_global_device_ids=true, to_apply=%region_57.63 | all-reduce | flops 256 | bytes 2048 | tf_op jit(solution)/shard_map/psum | solution.py:77
  (269 shorter events, 272.7 us)
Async XLA Ops:
  7.2 73.3 %copy-start.1 = (f32[4,64]{1,0:T(4,128)S(1)}, f32[4,64]{1,0:T(4,128)}, u32[]{:S(2)}) copy-start(f32[4,64]{1,0:T(4,128)} %param.14) | copy-start | bytes 3076
  7.2 7.6 copy-start
  7.2 148.4 %all-reduce.11.cloned.1.call-start = ((), (), s32[]{:S(2)}) async-start(), calls=%async_computation | async-start | bytes 524288 | tf_op jit(solution)/shard_map/psum | solution.py:53
  14.7 256.2 %all-reduce.13.cloned.1.call-start = ((), (), s32[]{:S(2)}) async-start(), calls=%async_computation.1 | async-start | bytes 524288 | tf_op jit(solution)/shard_map/psum | solution.py:64
  199.4 371.1 %all-reduce.15.cloned.1.call-start = ((), (), s32[]{:S(2)}) async-start(), calls=%async_computation.2 | async-start | bytes 524288 | tf_op jit(solution)/shard_map/psum | solution.py:53
  436.5 249.5 %all-reduce.17.cloned.1.call-start = ((), (), s32[]{:S(2)}) async-start(), calls=%async_computation.3 | async-start | bytes 524288 | tf_op jit(solution)/shard_map/psum | solution.py:64
  614.5 370.8 %all-reduce.19.cloned.1.call-start = ((), (), s32[]{:S(2)}) async-start(), calls=%async_computation.4 | async-start | bytes 524288 | tf_op jit(solution)/shard_map/psum | solution.py:53
  851.2 249.2 %all-reduce.21.cloned.1.call-start = ((), (), s32[]{:S(2)}) async-start(), calls=%async_computation.5 | async-start | bytes 524288 | tf_op jit(solution)/shard_map/psum | solution.py:64
  1029.0 371.0 %all-reduce.23.cloned.1.call-start = ((), (), s32[]{:S(2)}) async-start(), calls=%async_computation.6 | async-start | bytes 524288 | tf_op jit(solution)/shard_map/psum | solution.py:53
  1265.9 249.5 %all-reduce.25.cloned.1.call-start = ((), (), s32[]{:S(2)}) async-start(), calls=%async_computation.7 | async-start | bytes 524288 | tf_op jit(solution)/shard_map/psum | solution.py:64
  1443.9 370.8 %all-reduce.27.cloned.1.call-start = ((), (), s32[]{:S(2)}) async-start(), calls=%async_computation.8 | async-start | bytes 524288 | tf_op jit(solution)/shard_map/psum | solution.py:53
  1680.7 249.3 %all-reduce.29.cloned.1.call-start = ((), (), s32[]{:S(2)}) async-start(), calls=%async_computation.9 | async-start | bytes 524288 | tf_op jit(solution)/shard_map/psum | solution.py:64
Sparse Core Ops, SparseCore 0:
  14.8 140.7 all-reduce.10
  199.5 71.3 all-reduce.12
  436.6 133.8 all-reduce.14
  614.6 71.3 all-reduce.16
  851.4 133.8 all-reduce.18
  1029.1 71.3 all-reduce.20
  1266.0 133.8 all-reduce.22
  1444.1 71.3 all-reduce.24
  1680.8 133.8 all-reduce.26
  1858.6 71.3 all-reduce.28
where the time goes:
time: 2100 us; the launch traced here: 2090 us
  waiting for transfers between devices  900 us (43%)
  blocking collectives  859 us (41%)
  other arithmetic  196 us (9%)
  matrix products  90.9 us (4%)
  between operations  25.1 us (1%)
  local copies, waits for them, and re-layouts  22.6 us (1%)
    psum x5, waiting for transfers between devices, local(): sample_rhs = lax.psum(sample_terms, 'bld')  572 us
    psum x5, blocking collectives, local(): hour_rhs = lax.psum(hour_terms, ('smp', 'bld'))  337 us
    psum x5, waiting for transfers between devices, local(): build_rhs = lax.psum(build_terms, 'smp')  328 us
    psum x5, blocking collectives, local(): gram_raw = lax.psum(self_gram(unscaled), 'bld')  325 us
    psum x5, blocking collectives, local(): gram_raw = lax.psum(self_gram(unscaled), 'smp')  132 us
    another operation x45, other arithmetic, solve_rows(): lower_factor = jnp.linalg.cholesky(regularized(gram))  97.7 us
    another operation x30, other arithmetic, solve_rows(): lax.linalg.triangular_solve(lower_factor, middle, left_side=True, lower=T...  83.3 us
    psum x1, blocking collectives, local(): gram_build = lax.psum(self_gram(building_factor), 'bld')  65.3 us
  transfers between devices with their start and end apart: 10, of which 10 were waited for; matrix products, arithmetic and copies ran while one was open for 3% of the time, Pallas kernels for 0%

commit v1 on v0

--- a/solution.py
+++ b/solution.py
@@ -74,7 +74,7 @@
             "rj,kij->kri", build_low, tensor, preferred_element_type=jnp.float32
         )
         hour_terms = jnp.sum(sample_low.astype(jnp.float32)[None, :, :] * partial_value, axis=2)
-        hour_rhs = lax.psum(hour_terms, ("smp", "bld"))
+        hour_rhs = lax.psum(lax.psum(hour_terms, "bld"), "smp")
         hourly = solve_rows(gram_sample * gram_build, hour_rhs.T).T
     return (sample_out, building_out, hourly * scale_up)
 

time: 2100 us -> 2030 us (0.967)
  blocking collectives: 859 us -> 782 us
    psum x5 -> x10, blocking collectives: 337 us -> 261 us  [local(): hour_rhs = lax.psum(lax.psum(hour_terms, 'bld'), 'smp')]
where the time goes in v1:
time: 2030 us; the launch traced here: 2020 us
  waiting for transfers between devices  903 us (44%)
  blocking collectives  782 us (39%)
  other arithmetic  196 us (10%)
  matrix products  90.9 us (4%)
  between operations  25.4 us (1%)
  local copies, waits for them, and re-layouts  22.6 us (1%)
    psum x5, waiting for transfers between devices, local(): sample_rhs = lax.psum(sample_terms, 'bld')  575 us
    psum x5, waiting for transfers between devices, local(): build_rhs = lax.psum(build_terms, 'smp')  328 us
    psum x5, blocking collectives, local(): gram_raw = lax.psum(self_gram(unscaled), 'bld')  324 us
    psum x10, blocking collectives, local(): hour_rhs = lax.psum(lax.psum(hour_terms, 'bld'), 'smp')  261 us
    psum x5, blocking collectives, local(): gram_raw = lax.psum(self_gram(unscaled), 'smp')  132 us
    another operation x45, other arithmetic, solve_rows(): lower_factor = jnp.linalg.cholesky(regularized(gram))  97.7 us
    another operation x30, other arithmetic, solve_rows(): lax.linalg.triangular_solve(lower_factor, middle, left_side=True, lower=T...  83.3 us
    psum x1, blocking collectives, local(): gram_build = lax.psum(self_gram(building_factor), 'bld')  65.3 us
  transfers between devices with their start and end apart: 10, of which 10 were waited for; matrix products, arithmetic and copies ran while one was open for 3% of the time, Pallas kernels for 0%

profile of v1, /device:TPU:1, one launch (start us, length us, event | category | flops | bytes accessed | tf_op | source)
XLA Modules:
  0.0 2021.1 jit_solution(6296704623136235630)
XLA Ops:
  8.0 6.7 fusion.10
  15.2 65.3 %psum.217 = f32[64,64]{0,1:T(8,128)S(1)} all-reduce(f32[64,64]{0,1:T(8,128)S(1)} %fusion.159), channel_id=1, replica_groups=mesh['smp'=8,'bld'=16] {'bld'}, use_global_device_ids=true, to_apply=%region_0.0 | all-reduce | flops 4096 | bytes 32768 | tf_op jit(solution)/shard_map/psum | solution.py:46
  95.0 60.6 %all-reduce.11.cloned.1.call-done = f32[64,1024]{1,0:T(8,128)} async-done(((f32[64,1024]{1,0:T(8,128)}), f32[64,1024]{1,0:T(8,128)}) %all-reduce.11.cloned.1.call-update) | async-done | bytes 262160 | tf_op jit(solution)/shard_map/psum | solution.py:53
  157.7 26.2 %psum.219 = f32[64,64]{0,1:T(8,128)S(1)} all-reduce(f32[64,64]{0,1:T(8,128)S(1)} %fusion.160), channel_id=1, replica_groups=mesh['smp'=8,'bld'=16] {'smp'}, use_global_device_ids=true, to_apply=%region_6.10 | all-reduce | flops 4096 | bytes 32768 | tf_op jit(solution)/shard_map/psum | solution.py:55
  205.1 65.8 %all-reduce.13.cloned.1.call-done = f32[64,1024]{1,0:T(8,128)} async-done(((f32[64,1024]{1,0:T(8,128)}), f32[64,1024]{1,0:T(8,128)}) %all-reduce.13.cloned.1.call-update) | async-done | bytes 262160 | tf_op jit(solution)/shard_map/psum | solution.py:64
  273.0 65.0 %psum.221 = f32[64,64]{0,1:T(8,128)S(1)} all-reduce(f32[64,64]{0,1:T(8,128)S(1)} %fusion.161), channel_id=1, replica_groups=mesh['smp'=8,'bld'=16] {'bld'}, use_global_device_ids=true, to_apply=%region_10.14 | all-reduce | flops 4096 | bytes 32768 | tf_op jit(solution)/shard_map/psum | solution.py:66
  359.3 38.4 %psum.222 = f32[4,64]{1,0:T(4,128)S(1)} all-reduce(f32[4,64]{1,0:T(4,128)S(1)} %get-tuple-element.12), channel_id=1, replica_groups=mesh['smp'=8,'bld'=16] {'bld'}, use_global_device_ids=true, to_apply=%region_13.17 | all-reduce | flops 256 | bytes 2048 | tf_op jit(solution)/shard_map/psum | solution.py:77
  397.7 13.7 psum.223
  427.2 128.6 %all-reduce.15.cloned.1.call-done = f32[64,1024]{1,0:T(8,128)} async-done(((f32[64,1024]{1,0:T(8,128)}), f32[64,1024]{1,0:T(8,128)}) %all-reduce.15.cloned.1.call-update) | async-done | bytes 262160 | tf_op jit(solution)/shard_map/psum | solution.py:53
  557.9 26.2 %psum.225 = f32[64,64]{0,1:T(8,128)S(1)} all-reduce(f32[64,64]{0,1:T(8,128)S(1)} %fusion.162), channel_id=1, replica_groups=mesh['smp'=8,'bld'=16] {'smp'}, use_global_device_ids=true, to_apply=%region_18.24 | all-reduce | flops 4096 | bytes 32768 | tf_op jit(solution)/shard_map/psum | solution.py:55
  605.7 65.4 %all-reduce.17.cloned.1.call-done = f32[64,1024]{1,0:T(8,128)} async-done(((f32[64,1024]{1,0:T(8,128)}), f32[64,1024]{1,0:T(8,128)}) %all-reduce.17.cloned.1.call-update) | async-done | bytes 262160 | tf_op jit(solution)/shard_map/psum | solution.py:64
  673.2 64.7 %psum.227 = f32[64,64]{0,1:T(8,128)S(1)} all-reduce(f32[64,64]{0,1:T(8,128)S(1)} %fusion.163), channel_id=1, replica_groups=mesh['smp'=8,'bld'=16] {'bld'}, use_global_device_ids=true, to_apply=%region_22.28 | all-reduce | flops 4096 | bytes 32768 | tf_op jit(solution)/shard_map/psum | solution.py:66
  759.2 38.4 %psum.228 = f32[4,64]{1,0:T(4,128)S(1)} all-reduce(f32[4,64]{1,0:T(4,128)S(1)} %get-tuple-element.16), channel_id=1, replica_groups=mesh['smp'=8,'bld'=16] {'bld'}, use_global_device_ids=true, to_apply=%region_25.31 | all-reduce | flops 256 | bytes 2048 | tf_op jit(solution)/shard_map/psum | solution.py:77
  797.6 13.7 psum.229
  827.1 128.8 %all-reduce.19.cloned.1.call-done = f32[64,1024]{1,0:T(8,128)} async-done(((f32[64,1024]{1,0:T(8,128)}), f32[64,1024]{1,0:T(8,128)}) %all-reduce.19.cloned.1.call-update) | async-done | bytes 262160 | tf_op jit(solution)/shard_map/psum | solution.py:53
  958.0 26.5 %psum.231 = f32[64,64]{0,1:T(8,128)S(1)} all-reduce(f32[64,64]{0,1:T(8,128)S(1)} %fusion.164), channel_id=1, replica_groups=mesh['smp'=8,'bld'=16] {'smp'}, use_global_device_ids=true, to_apply=%region_30.36 | all-reduce | flops 4096 | bytes 32768 | tf_op jit(solution)/shard_map/psum | solution.py:55
  1005.7 65.8 %all-reduce.21.cloned.1.call-done = f32[64,1024]{1,0:T(8,128)} async-done(((f32[64,1024]{1,0:T(8,128)}), f32[64,1024]{1,0:T(8,128)}) %all-reduce.21.cloned.1.call-update) | async-done | bytes 262160 | tf_op jit(solution)/shard_map/psum | solution.py:64
  1073.6 64.7 %psum.233 = f32[64,64]{0,1:T(8,128)S(1)} all-reduce(f32[64,64]{0,1:T(8,128)S(1)} %fusion.165), channel_id=1, replica_groups=mesh['smp'=8,'bld'=16] {'bld'}, use_global_device_ids=true, to_apply=%region_34.40 | all-reduce | flops 4096 | bytes 32768 | tf_op jit(solution)/shard_map/psum | solution.py:66
  1159.6 38.4 %psum.234 = f32[4,64]{1,0:T(4,128)S(1)} all-reduce(f32[4,64]{1,0:T(4,128)S(1)} %get-tuple-element.20), channel_id=1, replica_groups=mesh['smp'=8,'bld'=16] {'bld'}, use_global_device_ids=true, to_apply=%region_37.43 | all-reduce | flops 256 | bytes 2048 | tf_op jit(solution)/shard_map/psum | solution.py:77
  1198.0 13.7 psum.235
  1227.7 128.4 %all-reduce.23.cloned.1.call-done = f32[64,1024]{1,0:T(8,128)} async-done(((f32[64,1024]{1,0:T(8,128)}), f32[64,1024]{1,0:T(8,128)}) %all-reduce.23.cloned.1.call-update) | async-done | bytes 262160 | tf_op jit(solution)/shard_map/psum | solution.py:53
  1358.2 26.2 %psum.237 = f32[64,64]{0,1:T(8,128)S(1)} all-reduce(f32[64,64]{0,1:T(8,128)S(1)} %fusion.166), channel_id=1, replica_groups=mesh['smp'=8,'bld'=16] {'smp'}, use_global_device_ids=true, to_apply=%region_42.48 | all-reduce | flops 4096 | bytes 32768 | tf_op jit(solution)/shard_map/psum | solution.py:55
  1405.6 65.8 %all-reduce.25.cloned.1.call-done = f32[64,1024]{1,0:T(8,128)} async-done(((f32[64,1024]{1,0:T(8,128)}), f32[64,1024]{1,0:T(8,128)}) %all-reduce.25.cloned.1.call-update) | async-done | bytes 262160 | tf_op jit(solution)/shard_map/psum | solution.py:64
  1473.4 64.7 %psum.239 = f32[64,64]{0,1:T(8,128)S(1)} all-reduce(f32[64,64]{0,1:T(8,128)S(1)} %fusion.167), channel_id=1, replica_groups=mesh['smp'=8,'bld'=16] {'bld'}, use_global_device_ids=true, to_apply=%region_46.52 | all-reduce | flops 4096 | bytes 32768 | tf_op jit(solution)/shard_map/psum | solution.py:66
  1559.5 38.4 %psum.240 = f32[4,64]{1,0:T(4,128)S(1)} all-reduce(f32[4,64]{1,0:T(4,128)S(1)} %get-tuple-element.24), channel_id=1, replica_groups=mesh['smp'=8,'bld'=16] {'bld'}, use_global_device_ids=true, to_apply=%region_49.55 | all-reduce | flops 256 | bytes 2048 | tf_op jit(solution)/shard_map/psum | solution.py:77
  1597.9 14.0 psum.241
  1627.6 128.6 %all-reduce.27.cloned.1.call-done = f32[64,1024]{1,0:T(8,128)} async-done(((f32[64,1024]{1,0:T(8,128)}), f32[64,1024]{1,0:T(8,128)}) %all-reduce.27.cloned.1.call-update) | async-done | bytes 262160 | tf_op jit(solution)/shard_map/psum | solution.py:53
  1758.4 26.5 %psum.243 = f32[64,64]{0,1:T(8,128)S(1)} all-reduce(f32[64,64]{0,1:T(8,128)S(1)} %fusion.168), channel_id=1, replica_groups=mesh['smp'=8,'bld'=16] {'smp'}, use_global_device_ids=true, to_apply=%region_54.60 | all-reduce | flops 4096 | bytes 32768 | tf_op jit(solution)/shard_map/psum | solution.py:55
  1806.7 64.9 %all-reduce.29.cloned.1.call-done = f32[64,1024]{1,0:T(8,128)} async-done(((f32[64,1024]{1,0:T(8,128)}), f32[64,1024]{1,0:T(8,128)}) %all-reduce.29.cloned.1.call-update) | async-done | bytes 262160 | tf_op jit(solution)/shard_map/psum | solution.py:64
  1873.7 65.0 %psum.245 = f32[64,64]{0,1:T(8,128)S(1)} all-reduce(f32[64,64]{0,1:T(8,128)S(1)} %fusion.169), channel_id=1, replica_groups=mesh['smp'=8,'bld'=16] {'bld'}, use_global_device_ids=true, to_apply=%region_58.64 | all-reduce | flops 4096 | bytes 32768 | tf_op jit(solution)/shard_map/psum | solution.py:66
  1960.1 38.4 %psum.246 = f32[4,64]{1,0:T(4,128)S(1)} all-reduce(f32[4,64]{1,0:T(4,128)S(1)} %bitcast.369), channel_id=1, replica_groups=mesh['smp'=8,'bld'=16] {'bld'}, use_global_device_ids=true, to_apply=%region_61.67 | all-reduce | flops 256 | bytes 2048 | tf_op jit(solution)/shard_map/psum | solution.py:77
  1998.5 13.7 psum.247
  (274 shorter events, 304.1 us)
Async XLA Ops:
  7.2 73.3 %copy-start.1 = (f32[4,64]{1,0:T(4,128)S(1)}, f32[4,64]{1,0:T(4,128)}, u32[]{:S(2)}) copy-start(f32[4,64]{1,0:T(4,128)} %param.14) | copy-start | bytes 3076
  7.2 7.6 copy-start
  7.2 148.4 %all-reduce.11.cloned.1.call-start = ((), (), s32[]{:S(2)}) async-start(), calls=%async_computation | async-start | bytes 524288 | tf_op jit(solution)/shard_map/psum | solution.py:53
  14.7 256.2 %all-reduce.13.cloned.1.call-start = ((), (), s32[]{:S(2)}) async-start(), calls=%async_computation.1 | async-start | bytes 524288 | tf_op jit(solution)/shard_map/psum | solution.py:64
  199.4 356.5 %all-reduce.15.cloned.1.call-start = ((), (), s32[]{:S(2)}) async-start(), calls=%async_computation.2 | async-start | bytes 524288 | tf_op jit(solution)/shard_map/psum | solution.py:53
  421.0 250.1 %all-reduce.17.cloned.1.call-start = ((), (), s32[]{:S(2)}) async-start(), calls=%async_computation.3 | async-start | bytes 524288 | tf_op jit(solution)/shard_map/psum | solution.py:64
  599.5 356.4 %all-reduce.19.cloned.1.call-start = ((), (), s32[]{:S(2)}) async-start(), calls=%async_computation.4 | async-start | bytes 524288 | tf_op jit(solution)/shard_map/psum | solution.py:53
  820.9 250.6 %all-reduce.21.cloned.1.call-start = ((), (), s32[]{:S(2)}) async-start(), calls=%async_computation.5 | async-start | bytes 524288 | tf_op jit(solution)/shard_map/psum | solution.py:64
  1000.0 356.2 %all-reduce.23.cloned.1.call-start = ((), (), s32[]{:S(2)}) async-start(), calls=%async_computation.6 | async-start | bytes 524288 | tf_op jit(solution)/shard_map/psum | solution.py:53
  1221.3 250.1 %all-reduce.25.cloned.1.call-start = ((), (), s32[]{:S(2)}) async-start(), calls=%async_computation.7 | async-start | bytes 524288 | tf_op jit(solution)/shard_map/psum | solution.py:64
  1399.8 356.4 %all-reduce.27.cloned.1.call-start = ((), (), s32[]{:S(2)}) async-start(), calls=%async_computation.8 | async-start | bytes 524288 | tf_op jit(solution)/shard_map/psum | solution.py:53
  1621.4 250.1 %all-reduce.29.cloned.1.call-start = ((), (), s32[]{:S(2)}) async-start(), calls=%async_computation.9 | async-start | bytes 524288 | tf_op jit(solution)/shard_map/psum | solution.py:64
Sparse Core Ops, SparseCore 0:
  14.8 140.7 all-reduce.10
  199.5 71.3 all-reduce.12
  421.1 134.7 all-reduce.14
  599.7 71.3 all-reduce.16
  821.0 134.9 all-reduce.18
  1000.1 71.3 all-reduce.20
  1221.4 134.7 all-reduce.22
  1400.0 71.3 all-reduce.24
  1621.5 134.7 all-reduce.26
  1800.5 70.9 all-reduce.28
